TPU v7x, 32 devices: a whole 2x2x4 slice. The times are simulated.
32 devices in a mesh: groups: 2 (over x), blk: 4 (over y, core), rows: 4 (over z).
Axes of the slice: x: 2, y: 2, z: 4, core: 2. Of those that a mesh axis runs over, the one named last changes fastest.
Arguments:
- tiles: float32 [64, 4, 4, 256, 256], P(('groups', 'rows'), 'blk'), parts along dimension 0, may hold values from 0 to 0.00078125
- tile_index: int32 [64, 4, 4], P(('groups', 'rows'), 'blk'), parts along dimension 0, may hold values from 0 to 7
- tiles_in_use: int32 [64, 4], P(('groups', 'rows'), 'blk'), parts along dimension 0, may hold values from 1 to 4, 10 in all within a row
- demand: int32 [128], P('groups'), parts along dimension 0, may hold values from 0 to 63, each once
- profiles: float32 [128, 8192], P('groups', 'blk'), parts along dimension 0, may hold values from 0.05 to 2.7, as said below
- capacity: float32 [128, 8192], P('groups', 'rows'), parts along dimension 0, may hold values from 0.05 to 4.5, as said below
- start_rates: float32 [128, 8192], P('groups', 'blk'), parts along dimension 0, may hold values from 0 to 1
- start_duals: float32 [128, 8192], P('groups', 'rows'), parts along dimension 0, may hold values from 0 to 1
- primal_weight: float32 [128], P('groups'), parts along dimension 0, may hold values from 0.5 to 2
Outputs:
- rates: float32 [128, 8192], P('groups', 'blk'), parts along dimension 0
- duals: float32 [128, 8192], P('groups', 'rows'), parts along dimension 0
- weight: float32 [128], P('groups'), parts along dimension 0
There are 2 independent parts, one for each index of `groups`. A program takes and returns all parts, laid end to end along the dimension named above; each array names one. Nothing has to cross between parts.
Inputs may be any that keep to these rules, and one draw needn't show every extreme that they name: `tile_index`: each slot names a link block inside its own column shard. `tiles_in_use`: for every row block the counts over the 4 column shards add up to 10, and the largest of them is 4. `demand`: each scenario names a different profile. `profiles`: positive weights. `capacity`: positive capacities.
All inputs are finite; a program needn't handle non-finite values.
Results may differ from a plain program's by a relative error of at most 0.00011.
Values sent between devices are 32-bit elements; how exact they have to be, the bound alone decides.
A program may use at most 64 MiB of HBM per device.

v0:
```python
import jax
import jax.numpy as jnp
from jax import lax
from jax.sharding import PartitionSpec as P

ITERS = 3


ETA = 0.9
EPS = 1e-06
exact_precision = lax.Precision.HIGHEST


def body(
    tiles,
    tile_index,
    tiles_in_use,
    demand,
    profiles,
    capacity,
    start_rates,
    start_duals,
    primal_weight,
):
    local_tiles = tiles[:, 0]
    local_columns = tile_index[:, 0]
    shard_tile_counts = tiles_in_use[:, 0]
    block_rows = local_tiles.shape[0]
    slot_count = local_tiles.shape[1]
    tile_width = local_tiles.shape[2]
    scen_count = profiles.shape[0]
    link_width = profiles.shape[1]
    column_blocks = link_width // tile_width
    dual_width = capacity.shape[1]
    blk_count = lax.axis_size("blk")
    rows_count = lax.axis_size("rows")
    total_links = link_width * blk_count
    total_rows = dual_width * rows_count
    dual_share = dual_width // blk_count
    blk_place = lax.axis_index("blk")
    slot_positions = lax.broadcasted_iota(jnp.int32, (block_rows, slot_count), 1)
    live_flags = (slot_positions < shard_tile_counts[:, None]).astype(jnp.float32)
    flat_columns = local_columns.reshape(-1)
    flattened_live = live_flags.reshape(-1)
    scen_iota = lax.broadcasted_iota(jnp.int32, (scen_count, scen_count), 1)
    selector = (demand[:, None] == scen_iota).astype(jnp.float32)
    utility_weights = jnp.dot(
        selector, profiles, precision=exact_precision, preferred_element_type=jnp.float32
    )
    block_iota = lax.broadcasted_iota(jnp.int32, (column_blocks, block_rows * slot_count), 0)
    scatter_table = (flat_columns[None, :] == block_iota).astype(jnp.float32) * flattened_live[
        None, :
    ]
    rates = start_rates
    duals = start_duals
    weight = primal_weight
    for iteration in range(ITERS):
        primal_step = ETA / weight
        dual_step = ETA * weight
        price_reshaped = duals.reshape(scen_count, block_rows, tile_width)
        contrib = jnp.einsum(
            "sri,rkij->srkj", price_reshaped, local_tiles, precision=exact_precision
        )
        contrib = contrib.reshape(scen_count, block_rows * slot_count, tile_width)
        result = jnp.einsum("cq,sqj->scj", scatter_table, contrib, precision=exact_precision)
        partial_grad = result.reshape(scen_count, link_width)
        primal_gradient = lax.psum(partial_grad, "rows") - utility_weights
        new_rates = jnp.clip(rates - primal_step[:, None] * primal_gradient, 0.0, 1.0)
        blended_rates = 2.0 * new_rates - rates
        link_view = blended_rates.reshape(scen_count, column_blocks, tile_width)
        picked = jnp.take(link_view, flat_columns, axis=1) * flattened_live[None, :, None]
        picked = picked.reshape(scen_count, block_rows, slot_count, tile_width)
        forward_result = jnp.einsum(
            "srkj,rkij->sri", picked, local_tiles, precision=exact_precision
        )
        dual_term = forward_result.reshape(scen_count, dual_width)
        old_share = lax.dynamic_slice_in_dim(duals, blk_place * dual_share, dual_share, 1)
        dual_piece = lax.psum_scatter(dual_term, "blk", scatter_dimension=1, tiled=True)
        capacity_share = lax.dynamic_slice_in_dim(capacity, blk_place * dual_share, dual_share, 1)
        new_share = jnp.maximum(0.0, old_share + dual_step[:, None] * (dual_piece - capacity_share))
        new_duals = lax.all_gather(new_share, "blk", axis=1, tiled=True)
        price_moves = jnp.sum((new_share - old_share) ** 2, axis=1)
        rate_delta = new_rates - rates
        rate_total = lax.psum(jnp.sum(rate_delta * rate_delta, axis=1), "blk")
        price_total = lax.psum(price_moves, ("blk", "rows"))
        move_x = jnp.sqrt(rate_total / total_links + EPS)
        move_y = jnp.sqrt(price_total / total_rows + EPS)
        weight = jnp.sqrt(weight * move_y / move_x)
        rates = new_rates
        duals = new_duals
    return (rates, duals, weight)


def solution(mesh):
    placed = (
        P(("groups", "rows"), "blk", None, None, None),
        P(("groups", "rows"), "blk", None),
        P(("groups", "rows"), "blk"),
        P("groups"),
        P("groups", "blk"),
        P("groups", "rows"),
        P("groups", "blk"),
        P("groups", "rows"),
        P("groups"),
    )
    return jax.shard_map(
        body,
        mesh=mesh,
        in_specs=placed,
        out_specs=(P("groups", "blk"), P("groups", "rows"), P("groups")),
        check_vma=False,
    )
```

profile of v0, /device:TPU:0, one launch (start us, length us, event | category | flops | bytes accessed | tf_op | source)
XLA Modules:
  0.0 340.9 jit_solution(16977567811629169493)
XLA Ops:
  10.1 8.0 %fusion.10 = f32[8,4,256,64]{2,3,1,0:T(8,128)S(1)} fusion(f32[8,1,4,256,256]{4,3,2,1,0:T(8,128)} %param.11, f32[64,8,256,1]{2,1,0,3:T(8,128)S(1)} %bitcast.128), kind=kOutput, calls=%fused_computation.13 | convolution fusion | flops 1610612736 | bytes 11010048 | tf_op jit(solution)/shard_map/sri,rkij->srkj/dot_general | solution.py:61
  18.1 2.4 fusion.16
  21.6 41.4 %all-reduce.4.cloned.1.call-done = f32[64,2048]{1,0:T(8,128)} async-done(((f32[64,2048]{1,0:T(8,128)}), f32[64,2048]{1,0:T(8,128)}) %all-reduce.4.cloned.1.call-update) | async-done | bytes 524304 | tf_op jit(solution)/shard_map/psum | solution.py:67
  63.0 2.4 multiply_reduce_fusion.2
  67.2 10.5 %fusion.18 = f32[8,8,8,256]{3,2,1,0:T(8,128)S(1)} fusion(f32[64,8,4,256]{3,0,2,1:T(8,128)S(1)} %bitcast.109, f32[8,1,4,256,256]{4,3,2,1,0:T(8,128)} %param.11), kind=kOutput, calls=%fused_computation.24 | convolution fusion | flops 1610612736 | bytes 11010048 | tf_op jit(solution)/shard_map/srkj,rkij->sri/dot_general | solution.py:73
  78.7 21.6 %reduce-scatter.4.cloned.1.call-done = f32[64,512]{1,0:T(8,128)} async-done(((f32[64,2048]{1,0:T(8,128)}), f32[64,512]{1,0:T(8,128)}) %reduce-scatter.4.cloned.1.call-update) | async-done | bytes 131088 | tf_op jit(solution)/shard_map/reduce_scatter | solution.py:78
  101.5 6.8 %all_gather.9 = f32[64,2048]{1,0:T(8,128)S(1)} all-gather(f32[64,512]{1,0:T(8,128)S(1)} %get-tuple-element.17), channel_id=1, replica_groups=mesh['groups'=2,'blk'=4,'rows'=4] {'blk'}, dimensions={1}, use_global_device_ids=true | all-gather | bytes 655360 | tf_op jit(solution)/shard_map/all_gather | solution.py:81
  109.1 7.5 %fusion.6 = f32[8,64,4,256]{3,1,2,0:T(8,128)S(1)} fusion(f32[8,1,4,256,256]{4,3,2,1,0:T(8,128)} %param.11, f32[64,8,256,1]{2,1,0,3:T(8,128)S(1)} %bitcast.129), kind=kOutput, calls=%fused_computation.9 | convolution fusion | flops 1610612736 | bytes 11010048 | tf_op jit(solution)/shard_map/sri,rkij->srkj/dot_general | solution.py:61
  116.6 2.4 fusion.14
  120.1 6.7 %psum.65 = f32[64]{0:T(128)S(1)} all-reduce(f32[64]{0:T(128)S(1)} %get-tuple-element.18), channel_id=1, replica_groups=mesh['groups'=2,'blk'=4,'rows'=4] {'blk'}, use_global_device_ids=true, to_apply=%region_5.7 | all-reduce | flops 64 | bytes 512 | tf_op jit(solution)/shard_map/psum | solution.py:84
  126.8 32.2 %psum.64 = f32[64]{0:T(128)S(1)} all-reduce(f32[64]{0:T(128)S(1)} %get-tuple-element.16), channel_id=1, replica_groups=mesh['groups'=2,'blk'=4,'rows'=4] {'blk','rows'}, use_global_device_ids=true, to_apply=%region_3.5 | all-reduce | flops 64 | bytes 512 | tf_op jit(solution)/shard_map/psum | solution.py:85
  159.6 1.3 multiply_reduce_fusion.1
  162.7 10.5 %fusion.21 = f32[8,8,8,256]{3,2,1,0:T(8,128)S(1)} fusion(f32[64,8,4,256]{3,0,2,1:T(8,128)S(1)} %bitcast.110, f32[8,1,4,256,256]{4,3,2,1,0:T(8,128)} %param.11), kind=kOutput, calls=%fused_computation.25 | convolution fusion | flops 1610612736 | bytes 11010048 | tf_op jit(solution)/shard_map/srkj,rkij->sri/dot_general | solution.py:73
  174.2 22.0 %reduce-scatter.6.cloned.1.call-done = f32[64,512]{1,0:T(8,128)} async-done(((f32[64,2048]{1,0:T(8,128)}), f32[64,512]{1,0:T(8,128)}) %reduce-scatter.6.cloned.1.call-update) | async-done | bytes 131088 | tf_op jit(solution)/shard_map/reduce_scatter | solution.py:78
  197.4 6.8 %all_gather.10 = f32[64,2048]{1,0:T(8,128)S(1)} all-gather(f32[64,512]{1,0:T(8,128)S(1)} %get-tuple-element.11), channel_id=1, replica_groups=mesh['groups'=2,'blk'=4,'rows'=4] {'blk'}, dimensions={1}, use_global_device_ids=true | all-gather | bytes 655360 | tf_op jit(solution)/shard_map/all_gather | solution.py:81
  205.0 7.5 %fusion.2 = f32[8,64,4,256]{3,1,2,0:T(8,128)S(1)} fusion(f32[8,1,4,256,256]{4,3,2,1,0:T(8,128)} %param.11, f32[64,8,256,1]{2,1,0,3:T(8,128)S(1)} %bitcast.130), kind=kOutput, calls=%fused_computation.5 | convolution fusion | flops 1610612736 | bytes 11010048 | tf_op jit(solution)/shard_map/sri,rkij->srkj/dot_general | solution.py:61
  212.6 2.4 fusion.12
  216.0 6.7 %psum.68 = f32[64]{0:T(128)S(1)} all-reduce(f32[64]{0:T(128)S(1)} %get-tuple-element.12), channel_id=1, replica_groups=mesh['groups'=2,'blk'=4,'rows'=4] {'blk'}, use_global_device_ids=true, to_apply=%region_11.13 | all-reduce | flops 64 | bytes 512 | tf_op jit(solution)/shard_map/psum | solution.py:84
  222.7 32.1 %psum.67 = f32[64]{0:T(128)S(1)} all-reduce(f32[64]{0:T(128)S(1)} %get-tuple-element.10), channel_id=1, replica_groups=mesh['groups'=2,'blk'=4,'rows'=4] {'blk','rows'}, use_global_device_ids=true, to_apply=%region_9.11 | all-reduce | flops 64 | bytes 512 | tf_op jit(solution)/shard_map/psum | solution.py:85
  258.7 10.5 %fusion.24 = f32[8,8,8,256]{3,2,1,0:T(8,128)S(1)} fusion(f32[64,8,4,256]{3,0,2,1:T(8,128)S(1)} %bitcast.108, f32[8,1,4,256,256]{4,3,2,1,0:T(8,128)} %param.11), kind=kOutput, calls=%fused_computation.26 | convolution fusion | flops 1610612736 | bytes 11010048 | tf_op jit(solution)/shard_map/srkj,rkij->sri/dot_general | solution.py:73
  270.1 5.8 %psum.71 = f32[64]{0:T(128)S(1)} all-reduce(f32[64]{0:T(128)S(1)} %get-tuple-element.6), channel_id=1, replica_groups=mesh['groups'=2,'blk'=4,'rows'=4] {'blk'}, use_global_device_ids=true, to_apply=%region_17.19 | all-reduce | flops 64 | bytes 512 | tf_op jit(solution)/shard_map/psum | solution.py:84
  275.9 16.3 %reduce-scatter.8.cloned.1.call-done = f32[64,512]{1,0:T(8,128)} async-done(((f32[64,2048]{1,0:T(8,128)}), f32[64,512]{1,0:T(8,128)}) %reduce-scatter.8.cloned.1.call-update) | async-done | bytes 131088 | tf_op jit(solution)/shard_map/reduce_scatter | solution.py:78
  293.4 32.2 %psum.70 = f32[64]{0:T(128)S(1)} all-reduce(f32[64]{0:T(128)S(1)} %get-tuple-element.4), channel_id=1, replica_groups=mesh['groups'=2,'blk'=4,'rows'=4] {'blk','rows'}, use_global_device_ids=true, to_apply=%region_15.17 | all-reduce | flops 64 | bytes 512 | tf_op jit(solution)/shard_map/psum | solution.py:85
  325.6 7.1 %all_gather.11 = f32[64,2048]{1,0:T(8,128)S(1)} all-gather(f32[64,512]{1,0:T(8,128)S(1)} %get-tuple-element.5), channel_id=1, replica_groups=mesh['groups'=2,'blk'=4,'rows'=4] {'blk'}, dimensions={1}, use_global_device_ids=true | all-gather | bytes 655360 | tf_op jit(solution)/shard_map/all_gather | solution.py:81
  (79 shorter events, 23.3 us)
Async XLA Ops:
  7.2 55.8 %copy-start = (f32[64,2048]{1,0:T(8,128)S(1)}, f32[64,2048]{1,0:T(8,128)}, u32[]{:S(2)}) copy-start(f32[64,2048]{1,0:T(8,128)} %param.15) | copy-start | bytes 1572868
  7.2 55.8 %all-reduce.4.cloned.1.call-start = ((), (), s32[]{:S(2)}) async-start(), calls=%async_computation.3 | async-start | bytes 1048576 | tf_op jit(solution)/shard_map/psum | solution.py:67
  18.1 3.5 %copy-start.11 = (f32[64]{0:T(128)S(1)}, f32[64]{0:T(128)}, u32[]{:S(2)}) copy-start(f32[64]{0:T(128)} %param.19) | copy-start | bytes 772
  18.1 44.9 %copy-start.9 = (f32[64,2048]{1,0:T(8,128)S(1)}, f32[64,2048]{1,0:T(8,128)}, u32[]{:S(2)}) copy-start(f32[64,2048]{1,0:T(8,128)} %param.17) | copy-start | bytes 1572868
  18.1 44.9 %copy-start.12 = (s32[64]{0:T(128)S(1)}, s32[64]{0:T(128)}, u32[]{:S(2)}) copy-start(s32[64]{0:T(128)} %param.14) | copy-start | bytes 772
  21.5 78.8 %reduce-scatter.4.cloned.1.call-start = ((), (), s32[]{:S(2)}) async-start(), calls=%async_computation.4 | async-start | bytes 655360 | tf_op jit(solution)/shard_map/reduce_scatter | solution.py:78
  65.4 0.8 copy-start.1
  78.6 81.0 %all-reduce.6.cloned.1.call-start = ((), (), s32[]{:S(2)}) async-start(), calls=%async_computation.5 | async-start | bytes 1048576 | tf_op jit(solution)/shard_map/psum | solution.py:67
  108.3 0.8 copy-start.8
  116.6 43.0 %copy-start.2 = (f32[64,2048]{1,0:T(8,128)S(1)}, f32[64,2048]{1,0:T(8,128)}, u32[]{:S(2)}) copy-start(f32[64,2048]{1,0:T(8,128)} %copy-done.1) | copy-start | bytes 1572868
  116.6 43.0 %copy-start.5 = (f32[64,2048]{1,0:T(8,128)S(1)}, f32[64,2048]{1,0:T(8,128)}, u32[]{:S(2)}) copy-start(f32[64,2048]{1,0:T(8,128)} %get-tuple-element.22) | copy-start | bytes 1572868
  120.0 76.2 %reduce-scatter.6.cloned.1.call-start = ((), (), s32[]{:S(2)}) async-start(), calls=%async_computation.6 | async-start | bytes 655360 | tf_op jit(solution)/shard_map/reduce_scatter | solution.py:78
  161.0 0.8 copy-start.3
  174.2 81.4 %all-reduce.8.cloned.1.call-start = ((), (), s32[]{:S(2)}) async-start(), calls=%async_computation.7 | async-start | bytes 1048576 | tf_op jit(solution)/shard_map/psum | solution.py:67
  204.2 0.8 copy-start.7
  212.6 43.0 %copy-start.4 = (f32[64,2048]{1,0:T(8,128)S(1)}, f32[64,2048]{1,0:T(8,128)}, u32[]{:S(2)}) copy-start(f32[64,2048]{1,0:T(8,128)} %copy-done.3) | copy-start | bytes 1572868
  212.6 43.0 %copy-start.6 = (f32[64,2048]{1,0:T(8,128)S(1)}, f32[64,2048]{1,0:T(8,128)}, u32[]{:S(2)}) copy-start(f32[64,2048]{1,0:T(8,128)} %get-tuple-element.22) | copy-start | bytes 1572868
  216.0 76.2 %reduce-scatter.8.cloned.1.call-start = ((), (), s32[]{:S(2)}) async-start(), calls=%async_computation.8 | async-start | bytes 655360 | tf_op jit(solution)/shard_map/reduce_scatter | solution.py:78
  256.9 0.8 copy-start.10
Sparse Core Ops, SparseCore 0:
  21.6 41.3 all-reduce.3
  78.7 21.4 reduce-scatter.3
  120.1 39.4 all-reduce.5
  174.3 21.8 reduce-scatter.5
  216.1 39.4 all-reduce.7
  270.2 21.8 reduce-scatter.7
where the time goes:
time: 341 us
  blocking collectives  137 us (40%)
  waiting for transfers between devices  103 us (30%)
  matrix products  64.1 us (19%)
  between operations  14.5 us (4%)
  local copies, waits for them, and re-layouts  14.3 us (4%)
  other arithmetic  8.69 us (3%)
    psum x3, blocking collectives, body(): price_total = lax.psum(price_moves, ('blk', 'rows'))  96.6 us
    reduce_scatter x3, waiting for transfers between devices, body(): lax.psum_scatter(dual_term, 'blk', scatter_dimension=1, tiled=True)  59.8 us
    psum x3, waiting for transfers between devices, body(): primal_gradient = lax.psum(partial_grad, 'rows') - utility_weights  42.7 us
    dot_general x3, matrix products, body(): jnp.einsum('srkj,rkij->sri', picked, local_tiles, precision=exact_precision)  31.6 us
    dot_general x3, matrix products, body(): jnp.einsum('sri,rkij->srkj', price_reshaped, local_tiles, precision=exact...  23 us
    all_gather x3, blocking collectives, body(): new_duals = lax.all_gather(new_share, 'blk', axis=1, tiled=True)  20.8 us
    psum x3, blocking collectives, body(): rate_total = lax.psum(jnp.sum(rate_delta * rate_delta, axis=1), 'blk')  19.2 us
    unnamed x34, local copies, waits for them, and re-layouts  9.39 us
  transfers between devices with their start and end apart: 6, of which 6 were waited for; matrix products, arithmetic and copies ran while one was open for 0% of the time, Pallas kernels for 0%

commit v1 on v0

v1 whole, which is shorter than its diff:
```python
import functools

import jax
import jax.numpy as jnp
from jax import lax
from jax.experimental import pallas as pl
from jax.experimental.pallas import tpu as pltpu
from jax.sharding import PartitionSpec as P

ITERS = 3
ETA = 0.9
EPS = 1e-06
GROUPS = 2
CHUNKS = 2
Y_CHUNKS = 1
F32 = jnp.float32
BF16 = jnp.bfloat16


def split(x):
    hi = x.astype(BF16)
    return hi, (x - hi.astype(F32)).astype(BF16)


def kernel(
    rows_n, blk_n,
    tiles, tile_index, tiles_in_use, demand, profiles, capacity, start_rates, start_duals, weight_in,
    rates, duals, weight_out,
    stage, w_hi, w_lo, utility, price_split, link_split, contrib,
    z_acc, z_up, z_dn, c_send, c_recv, c_fin, y_acc, y_up, y_dn, x_move, y_move,
    load_sem, z_us, z_ur, z_ds, z_dr, y_us, y_ur, y_ds, y_dr, c_ss, c_sr, f_ss, f_sr,
    xm_ss, xm_sr, ym_ss, ym_sr,
):
    block_rows, _, slots, tile, _ = tiles.shape
    scen = profiles.shape[0]
    width = profiles.shape[1]
    dual_width = capacity.shape[1]
    blocks = width // tile
    span = scen // GROUPS
    half_rows = block_rows // 2
    total_links = width * blk_n
    total_rows = dual_width * rows_n
    z_pos = lax.axis_index("rows")
    b_pos = lax.axis_index("blk")
    y_n = blk_n // 2
    y_pos = b_pos // 2
    core = lax.rem(b_pos, 2)
    sibling = {"blk": b_pos + 1 - 2 * core}

    loads = [pltpu.make_async_copy(tiles.at[r, 0], stage.at[r], load_sem.at[r]) for r in range(block_rows)]
    for load in loads:
        load.start()

    barrier = pltpu.get_barrier_semaphore()
    for d in range(1, rows_n):
        pl.semaphore_signal(barrier, inc=1, device_id={"rows": lax.rem(z_pos + d, rows_n)}, device_id_type=pl.DeviceIdType.MESH)
    for d in range(1, blk_n):
        pl.semaphore_signal(barrier, inc=1, device_id={"blk": lax.rem(b_pos + d, blk_n)}, device_id_type=pl.DeviceIdType.MESH)

    def copy(src, dst, ss, rs, device):
        return pltpu.make_async_remote_copy(
            src_ref=src, dst_ref=dst, send_sem=ss, recv_sem=rs, device_id=device, device_id_type=pl.DeviceIdType.MESH
        )

    pending = []

    class Line:
        def __init__(self, n, pos, device, acc, up, dn, us, ur, ds, dr, chunks, count):
            self.n, self.acc, self.up, self.dn = n, acc, up, dn
            self.us, self.ur, self.ds, self.dr = us, ur, ds, dr
            self.chunks, self.size = chunks, count // chunks
            half = n // 2
            left = pos < half
            self.end = (pos == 0) | (pos == n - 1)
            self.mid = (pos == half - 1) | (pos == half)
            self.inner = device(jnp.where(left, pos + 1, pos - 1))
            self.outer = device(jnp.clip(jnp.where(left, pos - 1, pos + 1), 0, n - 1))

        def view(self, ref, b, g):
            return ref.at[b, pl.ds(g * self.size, self.size)]

        def to_mid(self, b, g):
            s = b * self.chunks + g
            return copy(self.view(self.acc, b, g), self.view(self.dn, b, g), self.us.at[s], self.dr.at[s], self.inner)

        def to_in(self, b, g):
            s = b * self.chunks + g
            return copy(self.view(self.acc, b, g), self.view(self.up, b, g), self.us.at[s], self.ur.at[s], self.inner)

        def to_out(self, b, g):
            s = b * self.chunks + g
            return copy(self.view(self.dn, b, g), self.view(self.dn, b, g), self.ds.at[s], self.dr.at[s], self.outer)

        def add(self, out, one, two, b, g):
            rows = pl.ds(g * self.size, self.size)
            out[b, rows] = one[b, rows] + two[b, rows]

        def rise(self, b, g):
            if self.n == 2:
                self.to_mid(b, g).start()
                return

            @pl.when(jnp.logical_not(self.end))
            def _():
                self.to_in(b, g).wait_recv()
                self.add(self.acc, self.acc, self.up, b, g)

            @pl.when(self.mid)
            def _():
                self.to_mid(b, g).start()

            @pl.when(jnp.logical_not(self.mid))
            def _():
                self.to_in(b, g).start()

        def fall(self, b, g):
            self.to_mid(b, g).wait_recv()
            if self.n == 2:
                self.add(self.dn, self.acc, self.dn, b, g)
                return

            @pl.when(self.mid)
            def _():
                self.add(self.dn, self.acc, self.dn, b, g)

            @pl.when(jnp.logical_not(self.end))
            def _():
                self.to_out(b, g).start()

        def drain(self, b, g):
            self.to_in(b, g).wait_send()
            if self.n > 2:

                @pl.when(jnp.logical_not(self.end))
                def _():
                    self.to_out(b, g).wait_send()

    z_line = Line(rows_n, z_pos, lambda p: {"rows": p}, z_acc, z_up, z_dn, z_us, z_ur, z_ds, z_dr, CHUNKS, blocks)
    y_line = Line(y_n, y_pos, lambda p: {"blk": 2 * p + core}, y_acc, y_up, y_dn, y_us, y_ur, y_ds, y_dr, Y_CHUNKS, half_rows)

    def scen_rows(h):
        return slice(h * span, (h + 1) * span)

    def lanes(i):
        return slice(i * tile, (i + 1) * tile)

    def lane_of(i):
        return pl.ds(pl.multiple_of(i * tile, tile), tile)

    def move_copies(buf, ss, sr, axis, pos, n, b):
        return [
            copy(buf.at[b, 0], buf.at[b, d], ss.at[b * n + d], sr.at[b * n + d], {axis: lax.rem(pos + d, n)})
            for d in range(1, n)
        ]

    def send_moves(copies):
        for c in copies:
            c.start()
            pending.append(c)

    def sum_moves(buf, copies, pos, n, b):
        for c in copies:
            c.wait_recv()
        total = None
        for j in range(n):
            part = buf[b, lax.rem(pos - j + n, n)]
            total = part if total is None else total + part
        return jnp.sum(total, axis=1, keepdims=True)

    def x_copies(b):
        return move_copies(x_move, xm_ss, xm_sr, "blk", b_pos, blk_n, b)

    def y_copies(b):
        return move_copies(y_move, ym_ss, ym_sr, "rows", z_pos, rows_n, b)

    def fold(sq):
        out = sq[:, :128]
        for i in range(1, tile // 128):
            out = out + sq[:, i * 128:(i + 1) * 128]
        return out

    weights = [weight_in[scen_rows(h), :] for h in range(GROUPS)]

    def next_weight(it, h):
        b = it * GROUPS + h
        move_x = jnp.sqrt(sum_moves(x_move, x_copies(b), b_pos, blk_n, b) / total_links + EPS)
        move_y = jnp.sqrt(sum_moves(y_move, y_copies(b), z_pos, rows_n, b) / total_rows + EPS)
        weights[h] = jnp.sqrt(weights[h] * move_y / move_x)

    def adjoint(it, h):
        b = it * GROUPS + h
        source = start_duals if it == 0 else duals
        for r in range(block_rows):
            hi, lo = split(source[scen_rows(h), lanes(r)])
            price_split[r, :span] = hi
            price_split[r, span:] = lo

        @pl.loop(0, block_rows)
        def _(r):
            lhs = price_split[r]
            for k in range(slots):
                t = r * slots + k
                main = jnp.dot(lhs, w_hi[t], preferred_element_type=F32)
                rest = jnp.dot(lhs[:span], w_lo[t], preferred_element_type=F32)
                contrib[t] = main[:span] + (main[span:] + rest)

        @pl.loop(0, blocks)
        def _(c):
            total = None
            for r in range(block_rows):
                for k in range(slots):
                    own = jnp.where(tile_index[r, 0, k] == c, 1.0, 0.0).astype(F32)
                    term = contrib[r * slots + k] * own
                    total = term if total is None else total + term
            z_acc[b, c] = total

    def rise(it, h):
        for g in range(CHUNKS):
            z_line.rise(it * GROUPS + h, g)

    def primal(it, h):
        b = it * GROUPS + h
        if it:
            next_weight(it - 1, h)
        step = ETA / weights[h]
        source = start_rates if it == 0 else rates
        moves = None
        for g in range(CHUNKS):
            z_line.fall(b, g)
            for c in range(g * z_line.size, (g + 1) * z_line.size):
                old = source[scen_rows(h), lanes(c)]
                grad = z_dn[b, c] - utility[scen_rows(h), lanes(c)]
                new = jnp.clip(old - step * grad, 0.0, 1.0)
                delta = new - old
                part = fold(delta * delta)
                moves = part if moves is None else moves + part
                rates[scen_rows(h), lanes(c)] = new
                hi, lo = split(2.0 * new - old)
                link_split[c, :span] = hi
                link_split[c, span:] = lo
        x_move[b, 0] = moves
        send_moves(x_copies(b))

    def forward_row(r):
        main = rest = None
        dims = (((1,), (1,)), ((), ()))
        for k in range(slots):
            t = r * slots + k
            lhs = link_split[tile_index[r, 0, k]]
            m = lax.dot_general(lhs, w_hi[t], dims, preferred_element_type=F32)
            e = lax.dot_general(lhs[:span], w_lo[t], dims, preferred_element_type=F32)
            main = m if main is None else main + m
            rest = e if rest is None else rest + e
        return main[:span] + (main[span:] + rest)

    def c_copy(b):
        return copy(c_send.at[b], c_recv.at[b], c_ss.at[b], c_sr.at[b], sibling)

    def f_copy(b):
        return copy(y_dn.at[b], c_fin.at[b], f_ss.at[b], f_sr.at[b], sibling)

    def forward(it, h):
        b = it * GROUPS + h

        @pl.loop(0, half_rows)
        def _(i):
            c_send[b, i] = forward_row((1 - core) * half_rows + i)

        c_copy(b).start()
        pending.append(c_copy(b))

        @pl.loop(0, half_rows)
        def _(i):
            y_acc[b, i] = forward_row(core * half_rows + i)

    def core_sum(it, h):
        b = it * GROUPS + h
        c_copy(b).wait_recv()
        y_acc[b] = y_acc[b] + c_recv[b]
        for g in range(Y_CHUNKS):
            y_line.rise(b, g)

    def y_sum(it, h):
        b = it * GROUPS + h
        for g in range(Y_CHUNKS):
            y_line.fall(b, g)
        f_copy(b).start()
        pending.append(f_copy(b))

    def dual(it, h):
        b = it * GROUPS + h
        step = ETA * weights[h]
        source = start_duals if it == 0 else duals

        def part(first, arrived):
            moves = None
            for i in range(half_rows):
                where = lane_of(first + i)
                old = source[scen_rows(h), where]
                new = jnp.maximum(0.0, old + step * (arrived[b, i] - capacity[scen_rows(h), where]))
                delta = new - old
                piece = fold(delta * delta)
                moves = piece if moves is None else moves + piece
                duals[scen_rows(h), where] = new
            return moves

        own = part(core * half_rows, y_dn)
        f_copy(b).wait_recv()
        other = part((1 - core) * half_rows, c_fin)
        y_move[b, 0] = own + other
        send_moves(y_copies(b))

    @pl.loop(0, scen)
    def _(s):
        utility[pl.ds(s, 1), :] = profiles[pl.ds(demand[s], 1), :]

    for r in range(block_rows):
        loads[r].wait()

        @pl.loop(0, slots)
        def _(k):
            live = jnp.where(k < tiles_in_use[r, 0], 1.0, 0.0).astype(F32)
            hi, lo = split(stage[r, k] * live)
            w_hi[r * slots + k] = hi
            w_lo[r * slots + k] = lo

    pl.semaphore_wait(barrier, rows_n - 1 + blk_n - 1)

    hs = range(GROUPS)
    for h in hs:
        adjoint(0, h)
        rise(0, h)
    for it in range(ITERS):
        for h in hs:
            primal(it, h)
            forward(it, h)
            if h:
                y_sum(it, h - 1)
            core_sum(it, h)
        for h in hs:
            if h == GROUPS - 1:
                y_sum(it, h)
            dual(it, h)
            if it < ITERS - 1:
                adjoint(it + 1, h)
                rise(it + 1, h)
    for h in hs:
        next_weight(ITERS - 1, h)
        weight_out[scen_rows(h), :] = weights[h]

    for c in pending:
        c.wait_send()
    for b in range(ITERS * GROUPS):
        for g in range(CHUNKS):
            z_line.drain(b, g)
        for g in range(Y_CHUNKS):
            y_line.drain(b, g)


def body(tiles, tile_index, tiles_in_use, demand, profiles, capacity, start_rates, start_duals, primal_weight):
    rows_n = lax.axis_size("rows")
    blk_n = lax.axis_size("blk")
    block_rows, _, slots, tile, _ = tiles.shape
    scen, width = profiles.shape
    dual_width = capacity.shape[1]
    blocks = width // tile
    span = scen // GROUPS
    nb = ITERS * GROUPS
    half = block_rows // 2
    vmem = pl.BlockSpec(memory_space=pltpu.VMEM)
    smem = pl.BlockSpec(memory_space=pltpu.SMEM)
    dma = pltpu.SemaphoreType.DMA
    z_buf = pltpu.VMEM((nb, blocks, span, tile), F32)
    y_buf = pltpu.VMEM((nb, half, span, tile), F32)
    rates, duals, weight = pl.pallas_call(
        functools.partial(kernel, rows_n, blk_n),
        out_shape=(
            jax.ShapeDtypeStruct((scen, width), F32),
            jax.ShapeDtypeStruct((scen, dual_width), F32),
            jax.ShapeDtypeStruct((scen, 1), F32),
        ),
        in_specs=[pl.BlockSpec(memory_space=pl.ANY), smem, smem, smem, vmem, vmem, vmem, vmem, vmem],
        out_specs=(vmem, vmem, vmem),
        scratch_shapes=[
            pltpu.VMEM((block_rows, slots, tile, tile), F32),
            pltpu.VMEM((block_rows * slots, tile, tile), BF16),
            pltpu.VMEM((block_rows * slots, tile, tile), BF16),
            pltpu.VMEM((scen, width), F32),
            pltpu.VMEM((block_rows, 2 * span, tile), BF16),
            pltpu.VMEM((blocks, 2 * span, tile), BF16),
            pltpu.VMEM((block_rows * slots, span, tile), F32),
            z_buf, z_buf, z_buf,
            y_buf, y_buf, y_buf, y_buf, y_buf, y_buf,
            pltpu.VMEM((nb, blk_n, span, 128), F32),
            pltpu.VMEM((nb, rows_n, span, 128), F32),
            dma((block_rows,)),
            dma((nb * CHUNKS,)), dma((nb * CHUNKS,)), dma((nb * CHUNKS,)), dma((nb * CHUNKS,)),
            dma((nb * Y_CHUNKS,)), dma((nb * Y_CHUNKS,)), dma((nb * Y_CHUNKS,)), dma((nb * Y_CHUNKS,)),
            dma((nb,)), dma((nb,)), dma((nb,)), dma((nb,)),
            dma((nb * blk_n,)), dma((nb * blk_n,)), dma((nb * rows_n,)), dma((nb * rows_n,)),
        ],
        compiler_params=pltpu.CompilerParams(
            collective_id=0, has_side_effects=True, vmem_limit_bytes=60 * 1024 * 1024
        ),
    )(
        tiles, tile_index, tiles_in_use, demand, profiles, capacity, start_rates, start_duals,
        primal_weight[:, None],
    )
    return rates, duals, weight[:, 0]


def solution(mesh):
    placed = (
        P(("groups", "rows"), "blk", None, None, None),
        P(("groups", "rows"), "blk", None),
        P(("groups", "rows"), "blk"),
        P("groups"),
        P("groups", "blk"),
        P("groups", "rows"),
        P("groups", "blk"),
        P("groups", "rows"),
        P("groups"),
    )
    return jax.shard_map(
        body,
        mesh=mesh,
        in_specs=placed,
        out_specs=(P("groups", "blk"), P("groups", "rows"), P("groups")),
        check_vma=False,
    )
```

time: 341 us -> 134 us (0.39)
  blocking collectives: 137 us -> 0 us
  Pallas kernels: 0 us -> 123 us
  waiting for transfers between devices: 103 us -> 0 us
  matrix products: 64.1 us -> 0 us
  between operations: 14.5 us -> 0.64 us
  other arithmetic: 8.69 us -> 1.39 us
  local copies, waits for them, and re-layouts: 14.3 us -> 7.76 us
    pallas_call x0 -> x1, Pallas kernels: none -> 123 us  [body(): pl.pallas_call(functools.partial(kernel, rows_n, blk_n), out_shape=(jax.S...]
    psum x6 -> x0, blocking collectives: 116 us -> none  [the longest x3 96.6 us: body(): price_total = lax.psum(price_moves, ('blk', 'rows'))]
    dot_general x10 -> x0, matrix products: 64.1 us -> none  [the longest x3 31.6 us: body(): jnp.einsum('srkj,rkij->sri', picked, local_tiles, precision=exact_precision)]
    reduce_scatter x3 -> x0, waiting for transfers between devices: 59.8 us -> none  [body(): lax.psum_scatter(dual_term, 'blk', scatter_dimension=1, tiled=True)]
    psum x3 -> x0, waiting for transfers between devices: 42.7 us -> none  [body(): primal_gradient = lax.psum(partial_grad, 'rows') - utility_weights]
    all_gather x3 -> x0, blocking collectives: 20.8 us -> none  [body(): new_duals = lax.all_gather(new_share, 'blk', axis=1, tiled=True)]
    reduce_sum x5 -> x0, other arithmetic: 6.37 us -> none  [the longest x3 3.68 us: body(): price_moves = jnp.sum((new_share - old_share) ** 2, axis=1)]
    unnamed x34 -> x4, local copies, waits for them, and re-layouts: 9.39 us -> 6.41 us
  transfers between devices with their start and end apart: 6 -> 0, of which waited for: 6 -> 0; matrix products, arithmetic and copies ran while one was open for 0% -> 0% of each run, Pallas kernels for 0% -> 0%
where the time goes in v1:
time: 134 us; the launch traced here: 133 us
  Pallas kernels  123 us (92%)
  local copies, waits for them, and re-layouts  7.76 us (6%)
  other arithmetic  1.39 us (1%)
    pallas_call x1, Pallas kernels, body(): pl.pallas_call(functools.partial(kernel, rows_n, blk_n), out_shape=(jax.S...  123 us
    unnamed x4, local copies, waits for them, and re-layouts  6.41 us

profile of v1, /device:TPU:0, one launch (start us, length us, event | category | flops | bytes accessed | tf_op | source)
XLA Modules:
  0.0 133.2 jit_solution(8703609458379997427)
XLA Ops:
  0.6 1.3 %copy.15.tile_index = s32[8,1,4]{2,1,0:T(1,128)} copy(s32[8,1,4]{0,2,1:T(4,128)} %param.10) | data formatting | bytes 256 | tf_op args[1]
  2.0 1.3 copy.16.tiles_in_use
  3.3 1.4 %copy.17.weight_in = f32[64,1]{1,0:T(8,128)} copy(f32[64,1]{0,1:T(1,128)} %bitcast.1) | data formatting | bytes 512 | tf_op jit(solution)/shard_map/broadcast_in_dim | solution.py:407
  4.7 123.4 %shard_map.112 = (f32[64,2048]{1,0:T(8,128)}, f32[64,2048]{1,0:T(8,128)}, f32[64,1]{1,0:T(8,128)}) custom-call(f32[8,1,4,256,256]{4,3,2,1,0:T(8,128)} %tiles.1, s32[8,1,4]{2,1,0:T(1,128)} %copy.15.tile_index, s32[8,1]{1,0:T(8,128)} %copy.16.tiles_in_use, s32[64]{0:T(128)} %demand.1, f32[64,2048]{1,0:T(8,128)} %profiles.1, f32[64,2048]{1,0:T(8,128)} %capacity.1, ...), custom_call_target="tpu_custom_call" | custom-call | tf_op jit(solution)/shard_map/pallas_call | solution.py:375
  128.1 1.4 %reduce = f32[64]{0:T(128)} reduce(f32[64,1]{1,0:T(8,128)} %get-tuple-element.8, f32[]{:T(128)} %constant.3), dimensions={1}, to_apply=%get-tuple-element.8.reduce_sub_computation | reduce | bytes 516 | tf_op jit(solution)/shard_map/pallas_call | solution.py:375
  129.5 1.9 %copy.20 = f32[64,2048]{1,0:T(8,128)} copy(f32[64,2048]{1,0:T(8,128)} %get-tuple-element.12) | data formatting | bytes 1048576
  131.3 1.9 %copy.21 = f32[64,2048]{1,0:T(8,128)} copy(f32[64,2048]{1,0:T(8,128)} %get-tuple-element.13) | data formatting | bytes 1048576

commit v2 on v1

--- a/solution.py
+++ b/solution.py
@@ -11,7 +11,7 @@
 ETA = 0.9
 EPS = 1e-06
 GROUPS = 2
-CHUNKS = 2
+CHUNKS = 4
 Y_CHUNKS = 1
 F32 = jnp.float32
 BF16 = jnp.bfloat16
@@ -24,11 +24,11 @@
 
 def kernel(
     rows_n, blk_n,
-    tiles, tile_index, tiles_in_use, demand, profiles, capacity, start_rates, start_duals, weight_in,
+    tiles, tile_index_in, tiles_in_use_in, demand, profiles, capacity, start_rates, start_duals, weight_in,
     rates, duals, weight_out,
-    stage, w_hi, w_lo, utility, price_split, link_split, contrib,
+    stage, w_hi, w_lo, t_hi, t_lo, utility, weight_col, tile_index, tiles_in_use, link_split, contrib,
     z_acc, z_up, z_dn, c_send, c_recv, c_fin, y_acc, y_up, y_dn, x_move, y_move,
-    load_sem, z_us, z_ur, z_ds, z_dr, y_us, y_ur, y_ds, y_dr, c_ss, c_sr, f_ss, f_sr,
+    load_sem, table_sem, z_us, z_ur, z_ds, z_dr, y_us, y_ur, y_ds, y_dr, c_ss, c_sr, f_ss, f_sr,
     xm_ss, xm_sr, ym_ss, ym_sr,
 ):
     block_rows, _, slots, tile, _ = tiles.shape
@@ -48,7 +48,11 @@
     sibling = {"blk": b_pos + 1 - 2 * core}
 
     loads = [pltpu.make_async_copy(tiles.at[r, 0], stage.at[r], load_sem.at[r]) for r in range(block_rows)]
-    for load in loads:
+    tables = [
+        pltpu.make_async_copy(tile_index_in, tile_index, table_sem.at[0]),
+        pltpu.make_async_copy(tiles_in_use_in, tiles_in_use, table_sem.at[1]),
+    ]
+    for load in tables + loads:
         load.start()
 
     barrier = pltpu.get_barrier_semaphore()
@@ -95,9 +99,17 @@
             rows = pl.ds(g * self.size, self.size)
             out[b, rows] = one[b, rows] + two[b, rows]
 
+        def launch(self, b, g):
+            if self.n == 2:
+                self.to_mid(b, g).start()
+                return
+
+            @pl.when(self.end)
+            def _():
+                self.to_in(b, g).start()
+
         def rise(self, b, g):
             if self.n == 2:
-                self.to_mid(b, g).start()
                 return
 
             @pl.when(jnp.logical_not(self.end))
@@ -109,9 +121,11 @@
             def _():
                 self.to_mid(b, g).start()
 
-            @pl.when(jnp.logical_not(self.mid))
-            def _():
-                self.to_in(b, g).start()
+            if self.n > 4:
+
+                @pl.when(jnp.logical_not(self.mid | self.end))
+                def _():
+                    self.to_in(b, g).start()
 
         def fall(self, b, g):
             self.to_mid(b, g).wait_recv()
@@ -179,7 +193,7 @@
             out = out + sq[:, i * 128:(i + 1) * 128]
         return out
 
-    weights = [weight_in[scen_rows(h), :] for h in range(GROUPS)]
+    weights = []
 
     def next_weight(it, h):
         b = it * GROUPS + h
@@ -187,68 +201,77 @@
         move_y = jnp.sqrt(sum_moves(y_move, y_copies(b), z_pos, rows_n, b) / total_rows + EPS)
         weights[h] = jnp.sqrt(weights[h] * move_y / move_x)
 
-    def adjoint(it, h):
-        b = it * GROUPS + h
+    def price_rows(it, h, first, count):
         source = start_duals if it == 0 else duals
-        for r in range(block_rows):
-            hi, lo = split(source[scen_rows(h), lanes(r)])
-            price_split[r, :span] = hi
-            price_split[r, span:] = lo
-
-        @pl.loop(0, block_rows)
+
+        @pl.loop(first, first + count)
         def _(r):
-            lhs = price_split[r]
+            hi, lo = split(source[scen_rows(h), lane_of(r)])
+            lhs = jnp.concatenate([hi, lo], axis=0)
             for k in range(slots):
                 t = r * slots + k
                 main = jnp.dot(lhs, w_hi[t], preferred_element_type=F32)
-                rest = jnp.dot(lhs[:span], w_lo[t], preferred_element_type=F32)
+                rest = jnp.dot(hi, w_lo[t], preferred_element_type=F32)
                 contrib[t] = main[:span] + (main[span:] + rest)
 
-        @pl.loop(0, blocks)
-        def _(c):
-            total = None
-            for r in range(block_rows):
-                for k in range(slots):
-                    own = jnp.where(tile_index[r, 0, k] == c, 1.0, 0.0).astype(F32)
-                    term = contrib[r * slots + k] * own
-                    total = term if total is None else total + term
-            z_acc[b, c] = total
-
-    def rise(it, h):
+    def scatter(it, h):
+        b = it * GROUPS + h
         for g in range(CHUNKS):
-            z_line.rise(it * GROUPS + h, g)
-
-    def primal(it, h):
-        b = it * GROUPS + h
-        if it:
+
+            @pl.loop(g * z_line.size, (g + 1) * z_line.size)
+            def _(c):
+                total = None
+                for r in range(block_rows):
+                    for k in range(slots):
+                        own = jnp.where(tile_index[k, r] == c, 1.0, 0.0).astype(F32)
+                        term = contrib[r * slots + k] * own
+                        total = term if total is None else total + term
+                z_acc[b, c] = total
+
+            z_line.launch(b, g)
+
+    def rise(it, h, g):
+        z_line.rise(it * GROUPS + h, g)
+
+    moves_of = {}
+
+    def primal(it, h, g):
+        b = it * GROUPS + h
+        if it and g == 0:
             next_weight(it - 1, h)
         step = ETA / weights[h]
         source = start_rates if it == 0 else rates
-        moves = None
-        for g in range(CHUNKS):
-            z_line.fall(b, g)
-            for c in range(g * z_line.size, (g + 1) * z_line.size):
-                old = source[scen_rows(h), lanes(c)]
-                grad = z_dn[b, c] - utility[scen_rows(h), lanes(c)]
-                new = jnp.clip(old - step * grad, 0.0, 1.0)
-                delta = new - old
-                part = fold(delta * delta)
-                moves = part if moves is None else moves + part
-                rates[scen_rows(h), lanes(c)] = new
-                hi, lo = split(2.0 * new - old)
-                link_split[c, :span] = hi
-                link_split[c, span:] = lo
-        x_move[b, 0] = moves
-        send_moves(x_copies(b))
-
-    def forward_row(r):
+        z_line.fall(b, g)
+        moves = moves_of.get(b)
+        for c in range(g * z_line.size, (g + 1) * z_line.size):
+            old = source[scen_rows(h), lanes(c)]
+            grad = z_dn[b, c] - utility[scen_rows(h), lanes(c)]
+            new = jnp.clip(old - step * grad, 0.0, 1.0)
+            delta = new - old
+            part = fold(delta * delta)
+            moves = part if moves is None else moves + part
+            rates[scen_rows(h), lanes(c)] = new
+            hi, lo = split(2.0 * new - old)
+            link_split[h, c, :span] = hi
+            link_split[h, c, span:] = lo
+        moves_of[b] = moves
+        if g == CHUNKS - 1:
+            x_move[b, 0] = moves
+            send_moves(x_copies(b))
+
+    def transpose_rows(first, count):
+        @pl.loop(first * slots, (first + count) * slots)
+        def _(t):
+            t_hi[t] = w_hi[t].T
+            t_lo[t] = w_lo[t].T
+
+    def forward_row(h, r):
         main = rest = None
-        dims = (((1,), (1,)), ((), ()))
         for k in range(slots):
             t = r * slots + k
-            lhs = link_split[tile_index[r, 0, k]]
-            m = lax.dot_general(lhs, w_hi[t], dims, preferred_element_type=F32)
-            e = lax.dot_general(lhs[:span], w_lo[t], dims, preferred_element_type=F32)
+            lhs = link_split[h, tile_index[k, r]]
+            m = jnp.dot(lhs, t_hi[t], preferred_element_type=F32)
+            e = jnp.dot(lhs[:span], t_lo[t], preferred_element_type=F32)
             main = m if main is None else main + m
             rest = e if rest is None else rest + e
         return main[:span] + (main[span:] + rest)
@@ -259,24 +282,30 @@
     def f_copy(b):
         return copy(y_dn.at[b], c_fin.at[b], f_ss.at[b], f_sr.at[b], sibling)
 
-    def forward(it, h):
-        b = it * GROUPS + h
-
-        @pl.loop(0, half_rows)
+    def forward_far(it, h, first, count):
+        b = it * GROUPS + h
+
+        @pl.loop(first, first + count)
         def _(i):
-            c_send[b, i] = forward_row((1 - core) * half_rows + i)
-
-        c_copy(b).start()
-        pending.append(c_copy(b))
-
-        @pl.loop(0, half_rows)
+            c_send[b, i] = forward_row(h, (1 - core) * half_rows + i)
+
+        if first + count == half_rows:
+            c_copy(b).start()
+            pending.append(c_copy(b))
+
+    def forward_near(it, h, first, count):
+        b = it * GROUPS + h
+
+        @pl.loop(first, first + count)
         def _(i):
-            y_acc[b, i] = forward_row(core * half_rows + i)
+            y_acc[b, i] = forward_row(h, core * half_rows + i)
 
     def core_sum(it, h):
         b = it * GROUPS + h
         c_copy(b).wait_recv()
         y_acc[b] = y_acc[b] + c_recv[b]
+        for g in range(Y_CHUNKS):
+            y_line.launch(b, g)
         for g in range(Y_CHUNKS):
             y_line.rise(b, g)
 
@@ -313,40 +342,80 @@
     @pl.loop(0, scen)
     def _(s):
         utility[pl.ds(s, 1), :] = profiles[pl.ds(demand[s], 1), :]
+        weight_col[pl.ds(s, 1), :] = jnp.full((1, 128), weight_in[s], F32)
+
+    for h in range(GROUPS):
+        weights.append(weight_col[scen_rows(h), :1])
+    for table in tables:
+        table.wait()
 
     for r in range(block_rows):
         loads[r].wait()
 
         @pl.loop(0, slots)
         def _(k):
-            live = jnp.where(k < tiles_in_use[r, 0], 1.0, 0.0).astype(F32)
+            live = jnp.where(k < tiles_in_use[0, r], 1.0, 0.0).astype(F32)
             hi, lo = split(stage[r, k] * live)
             w_hi[r * slots + k] = hi
             w_lo[r * slots + k] = lo
 
     pl.semaphore_wait(barrier, rows_n - 1 + blk_n - 1)
 
-    hs = range(GROUPS)
-    for h in hs:
-        adjoint(0, h)
-        rise(0, h)
+    quarter = block_rows // 4
+    eighth = half_rows // 2
+    price_rows(0, 0, 0, block_rows)
+    scatter(0, 0)
+    price_rows(0, 1, 0, block_rows)
     for it in range(ITERS):
-        for h in hs:
-            primal(it, h)
-            forward(it, h)
-            if h:
-                y_sum(it, h - 1)
-            core_sum(it, h)
-        for h in hs:
-            if h == GROUPS - 1:
-                y_sum(it, h)
-            dual(it, h)
-            if it < ITERS - 1:
-                adjoint(it + 1, h)
-                rise(it + 1, h)
-    for h in hs:
+        rise(it, 0, 0)
+        scatter(it, 1)
+
+        def fill(i):
+            if it == 0:
+                transpose_rows(i * quarter, quarter)
+
+        fill(0)
+        rise(it, 0, 1)
+        fill(1)
+        rise(it, 0, 2)
+        primal(it, 0, 0)
+        fill(2)
+        rise(it, 0, 3)
+        primal(it, 0, 1)
+        fill(3)
+        rise(it, 1, 0)
+        primal(it, 0, 2)
+        primal(it, 0, 3)
+        forward_far(it, 0, 0, eighth)
+        rise(it, 1, 1)
+        forward_far(it, 0, eighth, eighth)
+        rise(it, 1, 2)
+        primal(it, 1, 0)
+        forward_near(it, 0, 0, eighth)
+        rise(it, 1, 3)
+        primal(it, 1, 1)
+        forward_near(it, 0, eighth, eighth)
+        core_sum(it, 0)
+        primal(it, 1, 2)
+        primal(it, 1, 3)
+        forward_far(it, 1, 0, half_rows)
+        forward_near(it, 1, 0, eighth)
+        y_sum(it, 0)
+        forward_near(it, 1, eighth, eighth)
+        core_sum(it, 1)
+        dual(it, 0)
+        last = it == ITERS - 1
+        if not last:
+            price_rows(it + 1, 0, 0, block_rows)
+        y_sum(it, 1)
+        if not last:
+            scatter(it + 1, 0)
+        dual(it, 1)
+        if not last:
+            price_rows(it + 1, 1, 0, block_rows)
+    for h in range(GROUPS):
         next_weight(ITERS - 1, h)
-        weight_out[scen_rows(h), :] = weights[h]
+        weight_out[scen_rows(h), :] = jnp.broadcast_to(weights[h], (span, 128))
 
     for c in pending:
         c.wait_send()
@@ -355,6 +424,15 @@
             z_line.drain(b, g)
         for g in range(Y_CHUNKS):
             y_line.drain(b, g)
+
+
+def finish(rates, duals, weight, rates_out, duals_out, weight_out):
+    rates_out[...] = rates[...]
+    duals_out[...] = duals[...]
+    scen = weight_out.shape[0]
+    shape = weight.shape
+    here = lax.broadcasted_iota(jnp.int32, shape, 0) == lax.broadcasted_iota(jnp.int32, shape, 1)
+    weight_out[...] = jnp.sum(jnp.where(here, weight[...], 0.0), axis=0)[:scen]
 
 
 def body(tiles, tile_index, tiles_in_use, demand, profiles, capacity, start_rates, start_duals, primal_weight):
@@ -369,7 +447,9 @@
     half = block_rows // 2
     vmem = pl.BlockSpec(memory_space=pltpu.VMEM)
     smem = pl.BlockSpec(memory_space=pltpu.SMEM)
+    hbm = pl.BlockSpec(memory_space=pl.ANY)
     dma = pltpu.SemaphoreType.DMA
+    w_buf = pltpu.VMEM((block_rows * slots, tile, tile), BF16)
     z_buf = pltpu.VMEM((nb, blocks, span, tile), F32)
     y_buf = pltpu.VMEM((nb, half, span, tile), F32)
     rates, duals, weight = pl.pallas_call(
@@ -377,23 +457,24 @@
         out_shape=(
             jax.ShapeDtypeStruct((scen, width), F32),
             jax.ShapeDtypeStruct((scen, dual_width), F32),
-            jax.ShapeDtypeStruct((scen, 1), F32),
+            jax.ShapeDtypeStruct((scen, 128), F32),
         ),
-        in_specs=[pl.BlockSpec(memory_space=pl.ANY), smem, smem, smem, vmem, vmem, vmem, vmem, vmem],
+        in_specs=[hbm, hbm, hbm, smem, vmem, vmem, vmem, vmem, smem],
         out_specs=(vmem, vmem, vmem),
         scratch_shapes=[
             pltpu.VMEM((block_rows, slots, tile, tile), F32),
-            pltpu.VMEM((block_rows * slots, tile, tile), BF16),
-            pltpu.VMEM((block_rows * slots, tile, tile), BF16),
+            w_buf, w_buf, w_buf, w_buf,
             pltpu.VMEM((scen, width), F32),
-            pltpu.VMEM((block_rows, 2 * span, tile), BF16),
-            pltpu.VMEM((blocks, 2 * span, tile), BF16),
+            pltpu.VMEM((scen, 128), F32),
+            pltpu.SMEM((slots, block_rows), jnp.int32),
+            pltpu.SMEM((1, block_rows), jnp.int32),
+            pltpu.VMEM((GROUPS, blocks, 2 * span, tile), BF16),
             pltpu.VMEM((block_rows * slots, span, tile), F32),
             z_buf, z_buf, z_buf,
             y_buf, y_buf, y_buf, y_buf, y_buf, y_buf,
             pltpu.VMEM((nb, blk_n, span, 128), F32),
             pltpu.VMEM((nb, rows_n, span, 128), F32),
-            dma((block_rows,)),
+            dma((block_rows,)), dma((2,)),
             dma((nb * CHUNKS,)), dma((nb * CHUNKS,)), dma((nb * CHUNKS,)), dma((nb * CHUNKS,)),
             dma((nb * Y_CHUNKS,)), dma((nb * Y_CHUNKS,)), dma((nb * Y_CHUNKS,)), dma((nb * Y_CHUNKS,)),
             dma((nb,)), dma((nb,)), dma((nb,)), dma((nb,)),
@@ -403,10 +484,19 @@
             collective_id=0, has_side_effects=True, vmem_limit_bytes=60 * 1024 * 1024
         ),
     )(
-        tiles, tile_index, tiles_in_use, demand, profiles, capacity, start_rates, start_duals,
-        primal_weight[:, None],
+        tiles, tile_index[:, 0].T, tiles_in_use.T, demand, profiles, capacity, start_rates, start_duals,
+        primal_weight,
     )
-    return rates, duals, weight[:, 0]
+    return pl.pallas_call(
+        finish,
+        out_shape=(
+            jax.ShapeDtypeStruct(rates.shape, F32),
+            jax.ShapeDtypeStruct(duals.shape, F32),
+            jax.ShapeDtypeStruct((scen,), F32),
+        ),
+        in_specs=[vmem, vmem, vmem],
+        out_specs=(vmem, vmem, vmem),
+    )(rates, duals, weight)
 
 
 def solution(mesh):

time: 134 us -> 108 us (0.81)
  Pallas kernels: 123 us -> 108 us
  local copies, waits for them, and re-layouts: 7.76 us -> 0 us
  other arithmetic: 1.39 us -> 0 us
    pallas_call x1, Pallas kernels: 123 us -> 105 us  [body(): pl.pallas_call(functools.partial(kernel, rows_n, blk_n), out_shape=(jax.S...]
    unnamed x4 -> x0, local copies, waits for them, and re-layouts: 6.41 us -> none
    pallas_call x0 -> x1, Pallas kernels: none -> 2.2 us  [body(): pl.pallas_call(finish, out_shape=(jax.ShapeDtypeStruct(rates.shape, F32),...]
    pallas_call x1 -> x0, other arithmetic: 1.39 us -> none  [body(): pl.pallas_call(functools.partial(kernel, rows_n, blk_n), out_shape=(jax.S...]
    broadcast_in_dim x1 -> x0, local copies, waits for them, and re-layouts: 1.36 us -> none  [body(): primal_weight[:, None]]
where the time goes in v2:
time: 108 us
  Pallas kernels  108 us (100%)
    pallas_call x1, Pallas kernels, body(): pl.pallas_call(functools.partial(kernel, rows_n, blk_n), out_shape=(jax.S...  105 us
    pallas_call x1, Pallas kernels, body(): pl.pallas_call(finish, out_shape=(jax.ShapeDtypeStruct(rates.shape, F32),...  2.2 us

profile of v2, /device:TPU:0, one launch (start us, length us, event | category | flops | bytes accessed | tf_op | source)
XLA Modules:
  0.0 108.2 jit_solution(6756329600540941169)
XLA Ops:
  0.6 105.4 %shard_map.112 = (f32[64,2048]{1,0:T(8,128)}, f32[64,2048]{1,0:T(8,128)}, f32[64,128]{1,0:T(8,128)}) custom-call(f32[8,1,4,256,256]{4,3,2,1,0:T(8,128)} %tiles.1, s32[4,8]{1,0:T(4,128)} %bitcast.4, s32[1,8]{1,0:T(1,128)} %bitcast.5, s32[64]{0:T(128)} %demand.1, f32[64,2048]{1,0:T(8,128)} %profiles.1, f32[64,2048]{1,0:T(8,128)} %capacity.1, ...), custom_call_target="tpu_custom_call" | custom-call | tf_op jit(solution)/shard_map/pallas_call | solution.py:455
  106.0 2.2 %shard_map.113 = (f32[64,2048]{1,0:T(8,128)}, f32[64,2048]{1,0:T(8,128)}, f32[64]{0:T(128)}) custom-call(f32[64,2048]{1,0:T(8,128)} %get-tuple-element.6.rates, f32[64,2048]{1,0:T(8,128)} %get-tuple-element.7.duals, f32[64,128]{1,0:T(8,128)} %get-tuple-element.8.weight), custom_call_target="tpu_custom_call" | custom-call | tf_op jit(solution)/shard_map/pallas_call | solution.py:490

commit v3 on v2

--- a/solution.py
+++ b/solution.py
@@ -12,7 +12,7 @@
 EPS = 1e-06
 GROUPS = 2
 CHUNKS = 4
-Y_CHUNKS = 1
+Y_CHUNKS = 2
 F32 = jnp.float32
 BF16 = jnp.bfloat16
 
@@ -276,45 +276,43 @@
             rest = e if rest is None else rest + e
         return main[:span] + (main[span:] + rest)
 
-    def c_copy(b):
-        return copy(c_send.at[b], c_recv.at[b], c_ss.at[b], c_sr.at[b], sibling)
-
-    def f_copy(b):
-        return copy(y_dn.at[b], c_fin.at[b], f_ss.at[b], f_sr.at[b], sibling)
-
-    def forward_far(it, h, first, count):
-        b = it * GROUPS + h
-
-        @pl.loop(first, first + count)
+    y_size = half_rows // Y_CHUNKS
+
+    def c_copy(b, g):
+        rows, s = pl.ds(g * y_size, y_size), b * Y_CHUNKS + g
+        return copy(c_send.at[b, rows], c_recv.at[b, rows], c_ss.at[s], c_sr.at[s], sibling)
+
+    def f_copy(b, g):
+        rows, s = pl.ds(g * y_size, y_size), b * Y_CHUNKS + g
+        return copy(y_dn.at[b, rows], c_fin.at[b, rows], f_ss.at[s], f_sr.at[s], sibling)
+
+    def forward_far(it, h, g):
+        b = it * GROUPS + h
+
+        @pl.loop(g * y_size, (g + 1) * y_size)
         def _(i):
             c_send[b, i] = forward_row(h, (1 - core) * half_rows + i)
 
-        if first + count == half_rows:
-            c_copy(b).start()
-            pending.append(c_copy(b))
-
-    def forward_near(it, h, first, count):
-        b = it * GROUPS + h
-
-        @pl.loop(first, first + count)
+        c_copy(b, g).start()
+        pending.append(c_copy(b, g))
+
+    def forward_near(it, h, g):
+        b = it * GROUPS + h
+
+        @pl.loop(g * y_size, (g + 1) * y_size)
         def _(i):
             y_acc[b, i] = forward_row(h, core * half_rows + i)
 
-    def core_sum(it, h):
-        b = it * GROUPS + h
-        c_copy(b).wait_recv()
-        y_acc[b] = y_acc[b] + c_recv[b]
-        for g in range(Y_CHUNKS):
-            y_line.launch(b, g)
-        for g in range(Y_CHUNKS):
-            y_line.rise(b, g)
-
-    def y_sum(it, h):
-        b = it * GROUPS + h
-        for g in range(Y_CHUNKS):
-            y_line.fall(b, g)
-        f_copy(b).start()
-        pending.append(f_copy(b))
+        c_copy(b, g).wait_recv()
+        y_line.add(y_acc, y_acc, c_recv, b, g)
+        y_line.launch(b, g)
+        y_line.rise(b, g)
+
+    def y_sum(it, h, g):
+        b = it * GROUPS + h
+        y_line.fall(b, g)
+        f_copy(b, g).start()
+        pending.append(f_copy(b, g))
 
     def dual(it, h):
         b = it * GROUPS + h
@@ -334,7 +332,8 @@
             return moves
 
         own = part(core * half_rows, y_dn)
-        f_copy(b).wait_recv()
+        for g in range(Y_CHUNKS):
+            f_copy(b, g).wait_recv()
         other = part((1 - core) * half_rows, c_fin)
         y_move[b, 0] = own + other
         send_moves(y_copies(b))
@@ -362,7 +361,6 @@
     pl.semaphore_wait(barrier, rows_n - 1 + blk_n - 1)
 
     quarter = block_rows // 4
-    eighth = half_rows // 2
     price_rows(0, 0, 0, block_rows)
     scatter(0, 0)
     price_rows(0, 1, 0, block_rows)
@@ -386,28 +384,29 @@
         rise(it, 1, 0)
         primal(it, 0, 2)
         primal(it, 0, 3)
-        forward_far(it, 0, 0, eighth)
+        forward_far(it, 0, 0)
         rise(it, 1, 1)
-        forward_far(it, 0, eighth, eighth)
+        forward_far(it, 0, 1)
         rise(it, 1, 2)
         primal(it, 1, 0)
-        forward_near(it, 0, 0, eighth)
+        forward_near(it, 0, 0)
         rise(it, 1, 3)
+        forward_near(it, 0, 1)
         primal(it, 1, 1)
-        forward_near(it, 0, eighth, eighth)
-        core_sum(it, 0)
         primal(it, 1, 2)
         primal(it, 1, 3)
-        forward_far(it, 1, 0, half_rows)
-        forward_near(it, 1, 0, eighth)
-        y_sum(it, 0)
-        forward_near(it, 1, eighth, eighth)
-        core_sum(it, 1)
+        forward_far(it, 1, 0)
+        y_sum(it, 0, 0)
+        forward_far(it, 1, 1)
+        y_sum(it, 0, 1)
+        forward_near(it, 1, 0)
+        forward_near(it, 1, 1)
         dual(it, 0)
         last = it == ITERS - 1
         if not last:
             price_rows(it + 1, 0, 0, block_rows)
-        y_sum(it, 1)
+        y_sum(it, 1, 0)
+        y_sum(it, 1, 1)
         if not last:
             scatter(it + 1, 0)
         dual(it, 1)
@@ -477,7 +476,7 @@
             dma((block_rows,)), dma((2,)),
             dma((nb * CHUNKS,)), dma((nb * CHUNKS,)), dma((nb * CHUNKS,)), dma((nb * CHUNKS,)),
             dma((nb * Y_CHUNKS,)), dma((nb * Y_CHUNKS,)), dma((nb * Y_CHUNKS,)), dma((nb * Y_CHUNKS,)),
-            dma((nb,)), dma((nb,)), dma((nb,)), dma((nb,)),
+            dma((nb * Y_CHUNKS,)), dma((nb * Y_CHUNKS,)), dma((nb * Y_CHUNKS,)), dma((nb * Y_CHUNKS,)),
             dma((nb * blk_n,)), dma((nb * blk_n,)), dma((nb * rows_n,)), dma((nb * rows_n,)),
         ],
         compiler_params=pltpu.CompilerParams(

time: 108 us -> 107 us (level)
  no operation moved by 1% of the time
where the time goes in v3:
time: 107 us
  Pallas kernels  107 us (100%)
    pallas_call x1, Pallas kernels, body(): pl.pallas_call(functools.partial(kernel, rows_n, blk_n), out_shape=(jax.S...  104 us
    pallas_call x1, Pallas kernels, body(): pl.pallas_call(finish, out_shape=(jax.ShapeDtypeStruct(rates.shape, F32),...  2.2 us

profile of v3, /device:TPU:0, one launch (start us, length us, event | category | flops | bytes accessed | tf_op | source)
XLA Modules:
  0.0 107.2 jit_solution(8323127875695119899)
XLA Ops:
  0.6 104.4 %shard_map.112 = (f32[64,2048]{1,0:T(8,128)}, f32[64,2048]{1,0:T(8,128)}, f32[64,128]{1,0:T(8,128)}) custom-call(f32[8,1,4,256,256]{4,3,2,1,0:T(8,128)} %tiles.1, s32[4,8]{1,0:T(4,128)} %bitcast.4, s32[1,8]{1,0:T(1,128)} %bitcast.5, s32[64]{0:T(128)} %demand.1, f32[64,2048]{1,0:T(8,128)} %profiles.1, f32[64,2048]{1,0:T(8,128)} %capacity.1, ...), custom_call_target="tpu_custom_call" | custom-call | tf_op jit(solution)/shard_map/pallas_call | solution.py:454
  105.0 2.2 %shard_map.113 = (f32[64,2048]{1,0:T(8,128)}, f32[64,2048]{1,0:T(8,128)}, f32[64]{0:T(128)}) custom-call(f32[64,2048]{1,0:T(8,128)} %get-tuple-element.6.rates, f32[64,2048]{1,0:T(8,128)} %get-tuple-element.7.duals, f32[64,128]{1,0:T(8,128)} %get-tuple-element.8.weight), custom_call_target="tpu_custom_call" | custom-call | tf_op jit(solution)/shard_map/pallas_call | solution.py:489
